TPU v7x, 32 devices: a whole 2x2x4 slice. The times are simulated.
32 devices in a mesh: expert: 2 (over y), dp: 4 (over z), section: 4 (over x, core).
Axes of the slice: x: 2, y: 2, z: 4, core: 2. Of those that a mesh axis runs over, the one named last changes fastest.
Arguments:
- tokens: bfloat16 [4096, 1280], P(('expert', 'dp', 'section')), may hold values from -6 to 6
- routes: int32 [4096, 1], P(('expert', 'dp', 'section')), may hold values from 0 to 7
- w_router: bfloat16 [1280, 8], replicated, may hold values from -0.15625 to 0.15625
- w_in: bfloat16 [8, 1280, 5120], P(('expert', 'section'), None, 'dp'), may hold values from -0.15625 to 0.15625
- w_out: bfloat16 [8, 5120, 1280], P(('expert', 'section'), 'dp'), may hold values from -0.078125 to 0.078125
- cotangent: bfloat16 [4096, 1280], P(('expert', 'dp', 'section')), may hold values from -6 to 6
Outputs:
- moe_out: bfloat16 [4096, 1280], P(('expert', 'dp', 'section'))
- router_grad: float32 [1280, 8], replicated
- grad_w_in: bfloat16 [8, 1280, 5120], P(('expert', 'section'), None, 'dp')
- grad_w_out: bfloat16 [8, 5120, 1280], P(('expert', 'section'), 'dp')
Inputs may be any that keep to these rules, and one draw needn't show every extreme that they name: `routes`: each token names one expert; every expert is named by some token.
All inputs are finite; a program needn't handle non-finite values.
Results may differ from a plain program's by a relative error of at most 0.019.
Values may be sent and summed in bfloat16 or wider, within the bound.
A program may use at most 64 MiB of HBM per device.

v0:
```python
import functools
import math

import jax
import jax.numpy as jnp
from jax import lax
from jax.experimental import pallas as pl
from jax.experimental.pallas import tpu as pltpu
from jax.sharding import PartitionSpec as P

MESH = pl.DeviceIdType.MESH
F32 = jnp.float32
BF16 = jnp.bfloat16


def round_up(value, unit):
    return -(-value // unit) * unit


def tile_of(extent):
    return 256 if extent % 256 == 0 else extent


def exchange_kernel(
    dims,
    tok_ref, route_ref, wr_ref, cot_ref, win_hbm, wout_hbm,
    moe_ref, router_ref, rows_out, cots_out, act_out, hg_out,
    win, wout, slots, arrived, rows, act, slope, hg, part, rx, back_send, back, vec, vec_z, vec_p,
    a_send, a_recv, z_right, z_left, z_recv, c_send, c_recv, b_send, b_recv,
    v_send, v_recv, p_send, p_recv, w_sem, o_sem,
):
    n_y, n_z, n_s, cap, capp, blk, n_c, scale = dims
    chk = blk // n_c
    n_p = n_y * n_s
    y, z, s = lax.axis_index("expert"), lax.axis_index("dp"), lax.axis_index("section")
    me = y * n_s + s
    tok_count, width = tok_ref.shape
    hidden = win.shape[1]
    padded = n_p * capp
    ft, dt = tile_of(hidden), tile_of(width)

    load_in = pltpu.make_async_copy(win_hbm, win, w_sem.at[0])
    load_out = pltpu.make_async_copy(wout_hbm, wout, w_sem.at[1])
    load_in.start()
    load_out.start()

    def plane_id(q):
        return (q // n_s, z, q % n_s)

    def peer(k):
        return lax.rem(me + k, n_p)

    def source(k):
        return lax.rem(me + n_p - k, n_p)

    barrier = pltpu.get_barrier_semaphore()

    @pl.loop(1, n_p)
    def _(k):
        pl.semaphore_signal(barrier, inc=1, device_id=plane_id(peer(k)), device_id_type=MESH)

    @pl.loop(1, n_z)
    def _(k):
        pl.semaphore_signal(
            barrier, inc=1, device_id=(y, lax.rem(z + k, n_z), s), device_id_type=MESH
        )

    route = route_ref[...]
    onehot = (route == lax.broadcasted_iota(jnp.int32, (n_p, tok_count), 0)).astype(F32)
    token_row = lax.broadcasted_iota(jnp.int32, (tok_count, tok_count), 0)
    token_col = lax.broadcasted_iota(jnp.int32, (tok_count, tok_count), 1)
    earlier = (token_row < token_col).astype(F32).astype(BF16)
    ahead = jnp.dot(onehot.astype(BF16), earlier, preferred_element_type=F32)
    rank = jnp.sum(ahead * onehot, axis=0, keepdims=True).astype(jnp.int32)
    place = jnp.where(rank < cap, route * capp + rank, padded)
    dispatch = (place == lax.broadcasted_iota(jnp.int32, (padded, tok_count), 0)).astype(F32).astype(BF16)
    slots[0] = jnp.dot(dispatch, tok_ref[...], preferred_element_type=F32).astype(BF16)

    pl.semaphore_wait(barrier, n_p - 1 + n_z - 1)

    def padded_rows(q):
        return pl.ds(pl.multiple_of(q * capp, 16), capp)

    def block(o):
        return pl.ds(pl.multiple_of(o * blk, 16), blk)

    def chunk(o, c):
        return pl.ds(pl.multiple_of(o * blk + c * chk, 16), chk)

    part_p = n_p // n_c
    first = me // part_p

    def nth(t):
        return lax.rem(first + t, n_c)

    def plane_copy(i, k):
        return pltpu.make_async_remote_copy(
            src_ref=slots.at[i, padded_rows(peer(k))],
            dst_ref=arrived.at[i, padded_rows(me)],
            send_sem=a_send.at[i, k],
            recv_sem=a_recv.at[i, k],
            device_id=plane_id(peer(k)),
            device_id_type=MESH,
        )

    def plane_arrival(i, k):
        return pltpu.make_async_remote_copy(
            src_ref=slots.at[i, padded_rows(me)],
            dst_ref=arrived.at[i, padded_rows(source(k))],
            send_sem=a_send.at[i, k],
            recv_sem=a_recv.at[i, k],
            device_id=plane_id(peer(k)),
            device_id_type=MESH,
        )

    def start_plane(i):
        @pl.loop(0, n_p)
        def _(t):
            q = nth(t // part_p) * part_p + lax.rem(me + t, part_p)

            @pl.when(q != me)
            def _():
                plane_copy(i, lax.rem(q + n_p - me, n_p)).start()

        arrived[i, padded_rows(me), :] = slots[i, padded_rows(me), :]

    start_plane(0)

    logits = lax.dot_general(
        wr_ref[...], tok_ref[...], (((1,), (1,)), ((), ())), preferred_element_type=F32
    )
    gate_row = jax.nn.sigmoid(jnp.sum(logits * onehot, axis=0, keepdims=True))
    gate = jnp.sum(jnp.where(token_row == token_col, gate_row, 0.0), axis=1, keepdims=True)
    gated = (gate * cot_ref[...].astype(F32)).astype(BF16)
    slots[1] = jnp.dot(dispatch, gated, preferred_element_type=F32).astype(BF16)
    start_plane(1)

    part_pad = padded // n_c
    dense = lax.broadcasted_iota(jnp.int32, (chk, part_pad), 0)
    compact = (
        lax.broadcasted_iota(jnp.int32, (chk, part_pad), 1)
        == lax.div(dense, cap) * capp + lax.rem(dense, cap)
    ).astype(F32).astype(BF16)
    dense_t = lax.broadcasted_iota(jnp.int32, (part_pad, chk), 1)
    expand = (
        lax.broadcasted_iota(jnp.int32, (part_pad, chk), 0)
        == lax.div(dense_t, cap) * capp + lax.rem(dense_t, cap)
    ).astype(F32).astype(BF16)
    def part_rows(c):
        return pl.ds(pl.multiple_of(c * part_pad, 16), part_pad)

    def line_copy(i, o, c, to, sems):
        return pltpu.make_async_remote_copy(
            src_ref=rows.at[i, chunk(o, c)],
            dst_ref=rows.at[i, chunk(o, c)],
            send_sem=sems.at[i, o * n_c + c],
            recv_sem=z_recv.at[i, o * n_c + c],
            device_id=(y, to, s),
            device_id_type=MESH,
        )

    def send_right(i, o, c):
        @pl.when(z + 1 < n_z)
        def _():
            line_copy(i, o, c, z + 1, z_right).start()

    def send_left(i, o, c):
        @pl.when(z > 0)
        def _():
            line_copy(i, o, c, z - 1, z_left).start()

    def own_chunk(i, c):
        @pl.loop(0, part_p)
        def _(r):
            q = c * part_p + r

            @pl.when(q != me)
            def _():
                plane_arrival(i, lax.rem(me + n_p - q, n_p)).wait_recv()

        rows[i, chunk(z, c), :] = jnp.dot(
            compact, arrived[i, part_rows(c), :], preferred_element_type=F32
        ).astype(BF16)

    def line_step(i, k, c):
        @pl.when(z - k >= 0)
        def _():
            line_copy(i, z - k, c, z, z_right).wait_recv()
            send_right(i, z - k, c)

        @pl.when(z + k < n_z)
        def _():
            line_copy(i, z + k, c, z, z_left).wait_recv()
            send_left(i, z + k, c)

    def chain_copy(o, c, to, slot):
        return pltpu.make_async_remote_copy(
            src_ref=part.at[chunk(o, c)],
            dst_ref=rx.at[chunk(slot, c)],
            send_sem=c_send.at[o * n_c + c],
            recv_sem=c_recv.at[slot * n_c + c],
            device_id=(y, to, s),
            device_id_type=MESH,
        )

    def chain_send(o, c):
        @pl.when(z > o)
        def _():
            chain_copy(o, c, z - 1, o).start()

        @pl.when(z < o)
        def _():
            chain_copy(o, c, z + 1, jnp.where(z + 1 == o, n_z, o)).start()

    def forward(at):
        @pl.loop(0, hidden // ft)
        def _(j):
            cols = pl.ds(pl.multiple_of(j * ft, ft), ft)
            pre = jnp.dot(rows[0, at, :], win[:, cols], preferred_element_type=F32)
            cdf = 0.5 * (1.0 + lax.erf(pre * (1.0 / math.sqrt(2.0))))
            act[at, cols] = (pre * cdf).astype(BF16)
            slope[at, cols] = cdf + pre * jnp.exp(-0.5 * pre * pre) * (
                1.0 / math.sqrt(2.0 * math.pi)
            )

        @pl.loop(0, width // dt)
        def _(j):
            cols = pl.ds(pl.multiple_of(j * dt, dt), dt)
            part[at, cols] = jnp.dot(
                act[at, :], wout[:, cols], preferred_element_type=F32
            ).astype(BF16)

    def backward(o):
        @pl.loop(0, hidden // ft)
        def _(j):
            cols = pl.ds(pl.multiple_of(j * ft, ft), ft)
            grad = lax.dot_general(
                rows[1, block(o), :], wout[cols, :], (((1,), (1,)), ((), ())),
                preferred_element_type=F32,
            )
            hg[block(o), cols] = (grad * slope[block(o), cols]).astype(BF16)

    low_end, high_end = z == 0, z == n_z - 1
    at_end = jnp.logical_or(low_end, high_end)
    inside = jnp.logical_and(z > 0, z < n_z - 1)

    @pl.loop(0, n_c)
    def _(t):
        own_chunk(0, nth(t))
        send_right(0, z, nth(t))
        send_left(0, z, nth(t))

    @pl.loop(0, n_c)
    def _(t):
        own_chunk(1, nth(t))

    load_in.wait()
    load_out.wait()
    forward(block(z))

    @pl.loop(1, n_z)
    def _(k):
        @pl.when(k == jnp.where(at_end, 1, max(n_z - 2, 1)))
        def _():
            @pl.loop(0, n_c)
            def _(u):
                send_right(1, z, nth(u))
                send_left(1, z, nth(u))

        @pl.loop(0, n_c)
        def _(t):
            c = nth(t)
            line_step(0, k, c)

            @pl.when(at_end)
            def _():
                o = jnp.where(high_end, z - k, z + k)
                forward(chunk(o, c))
                chain_send(o, c)


        @pl.when(jnp.logical_and(inside, z - k >= 0))
        def _():
            forward(block(z - k))

        @pl.when(jnp.logical_and(inside, z + k < n_z))
        def _():
            forward(block(z + k))

    outs = [
        pltpu.make_async_copy(rows.at[0], rows_out, o_sem.at[0]),
        pltpu.make_async_copy(act, act_out, o_sem.at[1]),
        pltpu.make_async_copy(rows.at[1], cots_out, o_sem.at[2]),
        pltpu.make_async_copy(hg, hg_out, o_sem.at[3]),
    ]
    outs[0].start()
    outs[1].start()
    backward(z)

    def chain_step(o):
        @pl.loop(0, n_c)
        def _(t):
            c = nth(t)
            chain_copy(o, c, z, o).wait_recv()
            part[chunk(o, c), :] = (
                part[chunk(o, c), :].astype(F32) + rx[chunk(o, c), :].astype(F32)
            ).astype(BF16)
            chain_send(o, c)

    def chain_low(k):
        @pl.when(jnp.logical_and(z - k >= 0, z < n_z - 1))
        def _():
            chain_step(z - k)

    def chain_high(k):
        @pl.when(jnp.logical_and(z + k < n_z, z > 0))
        def _():
            chain_step(z + k)

    upper = 2 * z >= n_z

    def cot_step(k):
        @pl.loop(0, n_c)
        def _(t):
            line_step(1, k, nth(t))

    @pl.loop(1, n_z - 1)
    def _(k):
        @pl.when(k < n_z - 2)
        def _():
            cot_step(k)

            @pl.when(at_end)
            def _():
                backward(jnp.where(high_end, z - k, z + k))

        @pl.when(upper)
        def _():
            chain_low(k)

        @pl.when(jnp.logical_not(upper))
        def _():
            chain_high(k)

    @pl.loop(1, n_z - 1)
    def _(k):
        @pl.when(upper)
        def _():
            chain_high(k)

        @pl.when(jnp.logical_not(upper))
        def _():
            chain_low(k)

    if n_z > 2:
        cot_step(n_z - 2)

    def back_copy(k, q, there):
        return pltpu.make_async_remote_copy(
            src_ref=back_send.at[padded_rows(q)], dst_ref=back.at[padded_rows(there)],
            send_sem=b_send.at[k], recv_sem=b_recv.at[k],
            device_id=plane_id(q), device_id_type=MESH,
        )

    @pl.loop(0, n_c)
    def _(t):
        c = nth(t)

        @pl.when(z < n_z - 1)
        def _():
            chain_copy(z, c, z, z).wait_recv()

        @pl.when(z > 0)
        def _():
            chain_copy(z, c, z, n_z).wait_recv()

        from_right = jnp.where(z < n_z - 1, rx[chunk(z, c), :].astype(F32), 0.0)
        from_left = jnp.where(z > 0, rx[chunk(n_z, c), :].astype(F32), 0.0)
        final = (part[chunk(z, c), :].astype(F32) + from_right + from_left).astype(BF16)
        back_send[part_rows(c), :] = jnp.dot(expand, final, preferred_element_type=F32).astype(BF16)
        part[chunk(z, c), :] = final

        @pl.loop(0, part_p)
        def _(r):
            q = c * part_p + r

            @pl.when(q != me)
            def _():
                back_copy(lax.rem(q + n_p - me, n_p), q, me).start()

    back[padded_rows(me), :] = back_send[padded_rows(me), :]

    own_rows = rows[0, block(z), :]
    row_logits = lax.dot_general(
        own_rows, wr_ref[...], (((1,), (1,)), ((), ())), preferred_element_type=F32
    )
    mine = (lax.broadcasted_iota(jnp.int32, row_logits.shape, 1) == me).astype(F32)
    row_gate = jax.nn.sigmoid(jnp.sum(row_logits * mine, axis=1, keepdims=True))
    inner = jnp.sum(
        rows[1, block(z), :].astype(F32) * part[block(z), :].astype(F32), axis=1, keepdims=True
    )
    vec[0] = jnp.sum(
        own_rows.astype(F32) * (inner * (1.0 - row_gate)), axis=0, keepdims=True
    )

    def vec_copy(k, slot):
        return pltpu.make_async_remote_copy(
            src_ref=vec.at[0], dst_ref=vec_z.at[slot], send_sem=v_send.at[k], recv_sem=v_recv.at[k],
            device_id=(y, lax.rem(z + k, n_z), s), device_id_type=MESH,
        )

    @pl.loop(1, n_z)
    def _(k):
        vec_copy(k, z).start()

    @pl.when(inside)
    def _():
        @pl.loop(1, n_z - 1)
        def _(k):
            @pl.when(z - k >= 0)
            def _():
                backward(z - k)

            @pl.when(z + k < n_z)
            def _():
                backward(z + k)

    if n_z > 2:
        @pl.when(at_end)
        def _():
            backward(jnp.where(high_end, 1, n_z - 2))

    vec_z[z] = vec[0]

    @pl.loop(1, n_z)
    def _(k):
        vec_copy(k, lax.rem(z + n_z - k, n_z)).wait_recv()

    vec_p[me] = jnp.sum(vec_z[...], axis=0) * scale

    def vec_plane(k, slot):
        return pltpu.make_async_remote_copy(
            src_ref=vec_p.at[me], dst_ref=vec_p.at[slot], send_sem=p_send.at[k], recv_sem=p_recv.at[k],
            device_id=plane_id(peer(k)), device_id_type=MESH,
        )

    @pl.loop(1, n_p)
    def _(k):
        vec_plane(k, me).start()

    @pl.loop(1, n_p)
    def _(k):
        back_copy(k, peer(k), source(k)).wait_recv()

    picked = lax.dot_general(
        dispatch, back[...], (((0,), (0,)), ((), ())), preferred_element_type=F32
    )
    moe_ref[...] = (gate * picked).astype(BF16)

    @pl.loop(0, n_c)
    def _(t):
        line_step(1, n_z - 1, nth(t))

    outs[2].start()

    @pl.when(at_end)
    def _():
        backward(jnp.where(high_end, 0, n_z - 1))

    outs[3].start()

    @pl.loop(1, n_p)
    def _(k):
        vec_plane(k, source(k)).wait_recv()

    router_ref[...] = vec_p[...]

    @pl.loop(1, n_p)
    def _(k):
        plane_copy(0, k).wait_send()
        plane_copy(1, k).wait_send()
        back_copy(k, peer(k), me).wait_send()
        vec_plane(k, me).wait_send()

    @pl.loop(1, n_z)
    def _(k):
        vec_copy(k, z).wait_send()

    @pl.loop(0, n_z)
    def _(o):
        @pl.loop(0, n_c)
        def _(c):
            @pl.when(jnp.logical_and(o <= z, z + 1 < n_z))
            def _():
                line_copy(0, o, c, z, z_right).wait_send()
                line_copy(1, o, c, z, z_right).wait_send()

            @pl.when(jnp.logical_and(o >= z, z > 0))
            def _():
                line_copy(0, o, c, z, z_left).wait_send()
                line_copy(1, o, c, z, z_left).wait_send()

            @pl.when(o != z)
            def _():
                chain_copy(o, c, z, o).wait_send()

    for out in outs:
        out.wait()


def shards(tokens, routes, w_router, w_in, w_out, cotangent):
    tok_count, width = tokens.shape
    n_experts = w_router.shape[1]
    n_y, n_z, n_s = lax.axis_size("expert"), lax.axis_size("dp"), lax.axis_size("section")
    n_p = n_y * n_s
    cap = max(2, 3 * tok_count // (4 * n_experts))
    scale = math.sqrt(n_experts / (tok_count * n_y * n_z * n_s))
    capp = round_up(cap, 16)
    blk = round_up(n_p * cap, 16)
    n_c = 2 if n_p % 2 == 0 and n_p * cap % 32 == 0 else 1
    padded = n_p * capp
    hidden = w_in.shape[2]
    total = n_z * blk
    vmem = pl.BlockSpec(memory_space=pltpu.VMEM)
    hbm = pl.BlockSpec(memory_space=pl.ANY)
    dma = pltpu.SemaphoreType.DMA
    moe, router, rows, cots, act, hg = pl.pallas_call(
        functools.partial(exchange_kernel, (n_y, n_z, n_s, cap, capp, blk, n_c, scale)),
        out_shape=(
            jax.ShapeDtypeStruct((tok_count, width), BF16),
            jax.ShapeDtypeStruct((n_p, 1, width), F32),
            jax.ShapeDtypeStruct((total, width), BF16),
            jax.ShapeDtypeStruct((total, width), BF16),
            jax.ShapeDtypeStruct((total, hidden), BF16),
            jax.ShapeDtypeStruct((total, hidden), BF16),
        ),
        in_specs=[vmem, vmem, vmem, vmem, hbm, hbm],
        out_specs=(vmem, vmem, hbm, hbm, hbm, hbm),
        scratch_shapes=[
            pltpu.VMEM((width, hidden), BF16),
            pltpu.VMEM((hidden, width), BF16),
            pltpu.VMEM((2, padded, width), BF16),
            pltpu.VMEM((2, padded, width), BF16),
            pltpu.VMEM((2, total, width), BF16),
            pltpu.VMEM((total, hidden), BF16),
            pltpu.VMEM((total, hidden), F32),
            pltpu.VMEM((total, hidden), BF16),
            pltpu.VMEM((total, width), BF16),
            pltpu.VMEM((total + blk, width), BF16),
            pltpu.VMEM((padded, width), BF16),
            pltpu.VMEM((padded, width), BF16),
            pltpu.VMEM((1, 1, width), F32),
            pltpu.VMEM((n_z, 1, width), F32),
            pltpu.VMEM((n_p, 1, width), F32),
            dma((2, n_p)), dma((2, n_p)),
            dma((2, n_z * n_c)), dma((2, n_z * n_c)), dma((2, n_z * n_c)),
            dma((n_z * n_c,)), dma(((n_z + 1) * n_c,)),
            dma((n_p,)), dma((n_p,)),
            dma((n_z,)), dma((n_z,)), dma((n_p,)), dma((n_p,)),
            dma((2,)), dma((4,)),
        ],
        compiler_params=pltpu.CompilerParams(
            collective_id=0, has_side_effects=True, vmem_limit_bytes=60 << 20
        ),
    )(tokens, routes.reshape(1, tok_count), w_router.T, cotangent, w_in[0], w_out[0])
    by_row = (((0,), (0,)), ((), ()))
    grad_in = (
        lax.dot_general(rows, hg, by_row, preferred_element_type=F32) * scale
    ).astype(BF16)
    grad_out = (
        lax.dot_general(act, cots, by_row, preferred_element_type=F32) * scale
    ).astype(BF16)
    return (moe, router[:, 0, :].T, grad_in[None], grad_out[None])


def solution(mesh):
    return jax.shard_map(
        shards,
        mesh=mesh,
        in_specs=(
            P(("expert", "dp", "section"), None),
            P(("expert", "dp", "section"), None),
            P(),
            P(("expert", "section"), None, "dp"),
            P(("expert", "section"), "dp", None),
            P(("expert", "dp", "section"), None),
        ),
        out_specs=(
            P(("expert", "dp", "section"), None),
            P(),
            P(("expert", "section"), None, "dp"),
            P(("expert", "section"), "dp", None),
        ),
        check_vma=False,
    )
```

profile of v0, /device:TPU:0, one launch (start us, length us, event | category | flops | bytes accessed | tf_op | source)
XLA Modules:
  0.0 74.9 jit_solution(11206737714356607345)
XLA Ops:
  0.6 63.2 %shard_map.93 = (bf16[128,1280]{1,0:T(8,128)(2,1)}, f32[8,1,1280]{2,1,0:T(1,128)}, bf16[384,1280]{1,0:T(8,128)(2,1)}, bf16[384,1280]{1,0:T(8,128)(2,1)}, bf16[38...) custom-call(bf16[128,1280]{1,0:T(8,128)(2,1)} %tok_ref.1, s32[1,128]{1,0:T(1,128)} %bitcast.21, bf16[8,1280]{1,0:T(8,128)(2,1)} %bitcast.20, ...), custom_call_target="tpu_custom_call" | custom-call | tf_op jit(solution)/shard_map/pallas_call | solution.py:527
  63.9 1.4 %copy.12 = f32[8,1,1280]{2,0,1:T(8,128)} copy(f32[8,1,1280]{2,1,0:T(1,128)} %get-tuple-element.11) | data formatting | bytes 81920
  65.3 0.0 copy-start.1
  65.3 0.0 copy-start.2
  65.3 5.2 %fusion.3 = bf16[1,1280,1280]{2,1,0:T(8,128)(2,1)} fusion(bf16[384,1280]{1,0:T(8,128)(2,1)} %get-tuple-element.12, bf16[384,1280]{1,0:T(8,128)(2,1)} %get-tuple-element.13), kind=kOutput, calls=%fused_computation.5 | convolution fusion | flops 1261568000 | bytes 5242880 | tf_op jit(solution)/shard_map/dot_general | solution.py:568
  70.5 0.0 copy-done.1
  70.5 0.0 copy-done.2
  70.5 0.0 copy-start
  70.5 3.6 %fusion.2 = bf16[1,1280,1280]{2,1,0:T(8,128)(2,1)} fusion(bf16[384,1280]{1,0:T(8,128)(2,1)S(1)} %copy-done.2, bf16[384,1280]{1,0:T(8,128)(2,1)S(1)} %copy-done.1), kind=kOutput, calls=%fused_computation.4 | convolution fusion | flops 1261568000 | bytes 5242880 | tf_op jit(solution)/shard_map/dot_general | solution.py:571
  74.2 0.0 copy-done
  74.2 0.7 copy.14
Async XLA Ops:
  65.3 5.3 %copy-start.1 = (bf16[384,1280]{1,0:T(8,128)(2,1)S(1)}, bf16[384,1280]{1,0:T(8,128)(2,1)}, u32[]{:S(2)}) copy-start(bf16[384,1280]{1,0:T(8,128)(2,1)} %get-tuple-element.15) | copy-start | bytes 2949124
  65.3 5.3 %copy-start.2 = (bf16[384,1280]{1,0:T(8,128)(2,1)S(1)}, bf16[384,1280]{1,0:T(8,128)(2,1)}, u32[]{:S(2)}) copy-start(bf16[384,1280]{1,0:T(8,128)(2,1)} %get-tuple-element.14) | copy-start | bytes 2949124
  70.5 3.6 %copy-start = (bf16[128,1280]{1,0:T(8,128)(2,1)S(1)}, bf16[128,1280]{1,0:T(8,128)(2,1)}, u32[]{:S(2)}) copy-start(bf16[128,1280]{1,0:T(8,128)(2,1)} %get-tuple-element.20) | copy-start | bytes 983044
where the time goes:
time: 75.1 us; the launch traced here: 74.9 us
  Pallas kernels  63.2 us (84%)
  matrix products  8.87 us (12%)
  local copies, waits for them, and re-layouts  2.13 us (3%)
    pallas_call x1, Pallas kernels, shards(): pl.pallas_call(functools.partial(exchange_kernel, (n_y, n_z, n_s, cap, ca...  63.2 us
    dot_general x1, matrix products, shards(): lax.dot_general(rows, hg, by_row, preferred_element_type=F32) * scale  5.25 us
    dot_general x1, matrix products, shards(): lax.dot_general(act, cots, by_row, preferred_element_type=F32) * scale  3.62 us
    unnamed x8, local copies, waits for them, and re-layouts  2.13 us

commit v1 on v0

--- a/solution.py
+++ b/solution.py
@@ -15,10 +15,6 @@
 
 def round_up(value, unit):
     return -(-value // unit) * unit
-
-
-def tile_of(extent):
-    return 256 if extent % 256 == 0 else extent
 
 
 def exchange_kernel(
@@ -35,9 +31,7 @@
     y, z, s = lax.axis_index("expert"), lax.axis_index("dp"), lax.axis_index("section")
     me = y * n_s + s
     tok_count, width = tok_ref.shape
-    hidden = win.shape[1]
     padded = n_p * capp
-    ft, dt = tile_of(hidden), tile_of(width)
 
     load_in = pltpu.make_async_copy(win_hbm, win, w_sem.at[0])
     load_out = pltpu.make_async_copy(wout_hbm, wout, w_sem.at[1])
@@ -182,20 +176,29 @@
             compact, arrived[i, part_rows(c), :], preferred_element_type=F32
         ).astype(BF16)
 
-    def line_step(i, k, c):
-        @pl.when(z - k >= 0)
-        def _():
-            line_copy(i, z - k, c, z, z_right).wait_recv()
-            send_right(i, z - k, c)
-
-        @pl.when(z + k < n_z)
-        def _():
-            line_copy(i, z + k, c, z, z_left).wait_recv()
-            send_left(i, z + k, c)
-
-    def chain_copy(o, c, to, slot):
+    left_count, right_count = z, n_z - 1 - z
+
+    def relay(s_at, c):
+        @pl.when(jnp.logical_and(s_at >= 1, s_at <= 2 * left_count))
+        def _():
+            i = (s_at > left_count).astype(jnp.int32)
+            o = z - s_at + i * left_count
+            line_copy(i, o, c, z, z_right).wait_recv()
+            send_right(i, o, c)
+
+        @pl.when(jnp.logical_and(s_at >= 1, s_at <= 2 * right_count))
+        def _():
+            i = (s_at > right_count).astype(jnp.int32)
+            o = z + s_at - i * right_count
+            line_copy(i, o, c, z, z_left).wait_recv()
+            send_left(i, o, c)
+
+    low_end, high_end = z == 0, z == n_z - 1
+    at_end = jnp.logical_or(low_end, high_end)
+
+    def chain_copy(src, o, c, to, slot):
         return pltpu.make_async_remote_copy(
-            src_ref=part.at[chunk(o, c)],
+            src_ref=src.at[chunk(o, c)],
             dst_ref=rx.at[chunk(slot, c)],
             send_sem=c_send.at[o * n_c + c],
             recv_sem=c_recv.at[slot * n_c + c],
@@ -203,46 +206,57 @@
             device_id_type=MESH,
         )
 
-    def chain_send(o, c):
+    def chain_send(src, o, c):
         @pl.when(z > o)
         def _():
-            chain_copy(o, c, z - 1, o).start()
+            chain_copy(src, o, c, z - 1, o).start()
 
         @pl.when(z < o)
         def _():
-            chain_copy(o, c, z + 1, jnp.where(z + 1 == o, n_z, o)).start()
-
-    def forward(at):
-        @pl.loop(0, hidden // ft)
-        def _(j):
-            cols = pl.ds(pl.multiple_of(j * ft, ft), ft)
-            pre = jnp.dot(rows[0, at, :], win[:, cols], preferred_element_type=F32)
-            cdf = 0.5 * (1.0 + lax.erf(pre * (1.0 / math.sqrt(2.0))))
-            act[at, cols] = (pre * cdf).astype(BF16)
-            slope[at, cols] = cdf + pre * jnp.exp(-0.5 * pre * pre) * (
-                1.0 / math.sqrt(2.0 * math.pi)
-            )
-
-        @pl.loop(0, width // dt)
-        def _(j):
-            cols = pl.ds(pl.multiple_of(j * dt, dt), dt)
-            part[at, cols] = jnp.dot(
-                act[at, :], wout[:, cols], preferred_element_type=F32
-            ).astype(BF16)
-
-    def backward(o):
-        @pl.loop(0, hidden // ft)
-        def _(j):
-            cols = pl.ds(pl.multiple_of(j * ft, ft), ft)
-            grad = lax.dot_general(
-                rows[1, block(o), :], wout[cols, :], (((1,), (1,)), ((), ())),
-                preferred_element_type=F32,
-            )
-            hg[block(o), cols] = (grad * slope[block(o), cols]).astype(BF16)
-
-    low_end, high_end = z == 0, z == n_z - 1
-    at_end = jnp.logical_or(low_end, high_end)
-    inside = jnp.logical_and(z > 0, z < n_z - 1)
+            chain_copy(src, o, c, z + 1, jnp.where(z + 1 == o, n_z, o)).start()
+
+    def forward(o):
+        at = block(o)
+        pre = jnp.dot(rows[0, at, :], win[...], preferred_element_type=F32)
+        cdf = 0.5 * (1.0 + lax.erf(pre * (1.0 / math.sqrt(2.0))))
+        act[at, :] = (pre * cdf).astype(BF16)
+        slope[at, :] = cdf + pre * jnp.exp(-0.5 * pre * pre) * (1.0 / math.sqrt(2.0 * math.pi))
+        part[at, :] = jnp.dot(act[at, :], wout[...], preferred_element_type=F32).astype(BF16)
+
+    def backward():
+        grad = lax.dot_general(
+            rows[1], wout[...], (((1,), (1,)), ((), ())), preferred_element_type=F32
+        )
+        hg[...] = (grad * slope[...]).astype(BF16)
+
+    def router_terms(o):
+        own_rows = rows[0, block(o), :]
+        row_logits = lax.dot_general(
+            own_rows, wr_ref[...], (((1,), (1,)), ((), ())), preferred_element_type=F32
+        )
+        mine = (lax.broadcasted_iota(jnp.int32, row_logits.shape, 1) == me).astype(F32)
+        row_gate = jax.nn.sigmoid(jnp.sum(row_logits * mine, axis=1, keepdims=True))
+        inner = jnp.sum(
+            rows[1, block(o), :].astype(F32) * part[block(o), :].astype(F32), axis=1, keepdims=True
+        )
+        vec[0] = vec[0] + jnp.sum(
+            own_rows.astype(F32) * (inner * (1.0 - row_gate)), axis=0, keepdims=True
+        )
+
+    def send_cots(to_right, to_left):
+        @pl.when(to_right)
+        def _():
+            @pl.loop(0, n_c)
+            def _(t):
+                send_right(1, z, nth(t))
+
+        @pl.when(to_left)
+        def _():
+            @pl.loop(0, n_c)
+            def _(t):
+                send_left(1, z, nth(t))
+
+    vec[...] = jnp.zeros_like(vec)
 
     @pl.loop(0, n_c)
     def _(t):
@@ -250,42 +264,60 @@
         send_right(0, z, nth(t))
         send_left(0, z, nth(t))
 
-    @pl.loop(0, n_c)
-    def _(t):
-        own_chunk(1, nth(t))
-
     load_in.wait()
     load_out.wait()
-    forward(block(z))
-
-    @pl.loop(1, n_z)
-    def _(k):
-        @pl.when(k == jnp.where(at_end, 1, max(n_z - 2, 1)))
-        def _():
-            @pl.loop(0, n_c)
-            def _(u):
-                send_right(1, z, nth(u))
-                send_left(1, z, nth(u))
-
+
+    @pl.loop(0, 2 * n_z - 1)
+    def _(k):
         @pl.loop(0, n_c)
         def _(t):
-            c = nth(t)
-            line_step(0, k, c)
-
-            @pl.when(at_end)
-            def _():
-                o = jnp.where(high_end, z - k, z + k)
-                forward(chunk(o, c))
-                chain_send(o, c)
-
-
-        @pl.when(jnp.logical_and(inside, z - k >= 0))
-        def _():
-            forward(block(z - k))
-
-        @pl.when(jnp.logical_and(inside, z + k < n_z))
-        def _():
-            forward(block(z + k))
+            relay(k, nth(t))
+
+        send_cots(
+            jnp.logical_and(k >= 1, k == left_count), jnp.logical_and(k >= 1, k == right_count)
+        )
+
+        @pl.loop(0, 2)
+        def _(side):
+            o = jnp.where(side == 0, z - k, z + k)
+
+            @pl.when(jnp.logical_and(jnp.logical_and(o >= 0, o < n_z), k + 1 - side > 0))
+            def _():
+                forward(o)
+
+            @pl.when(jnp.logical_and(at_end, jnp.logical_and(o >= 0, o < n_z)))
+            def _():
+                @pl.loop(0, n_c)
+                def _(t):
+                    @pl.when(k >= 2)
+                    def _():
+                        chain_send(part, o, nth(t))
+
+                @pl.when(k == n_z - 1)
+                def _():
+                    @pl.loop(0, n_c)
+                    def _(t):
+                        chain_send(part, jnp.where(low_end, 1, n_z - 2), nth(t))
+
+        @pl.when(k == 0)
+        def _():
+            @pl.loop(0, n_c)
+            def _(t):
+                own_chunk(1, nth(t))
+
+        send_cots(
+            jnp.logical_and(k == 0, left_count == 0), jnp.logical_and(k == 0, right_count == 0)
+        )
+
+        @pl.loop(0, 2)
+        def _(side):
+            count = jnp.where(side == 0, left_count, right_count)
+            o = jnp.where(side == 0, z - k + count, z + k - count)
+            arrived_now = jnp.logical_and(k > count, k <= 2 * count)
+
+            @pl.when(jnp.logical_or(arrived_now, jnp.logical_and(k == 0, side == 0)))
+            def _():
+                router_terms(jnp.where(k == 0, z, o))
 
     outs = [
         pltpu.make_async_copy(rows.at[0], rows_out, o_sem.at[0]),
@@ -295,65 +327,64 @@
     ]
     outs[0].start()
     outs[1].start()
-    backward(z)
+    outs[2].start()
+
+    def vec_copy(k, slot):
+        return pltpu.make_async_remote_copy(
+            src_ref=vec.at[0], dst_ref=vec_z.at[slot], send_sem=v_send.at[k], recv_sem=v_recv.at[k],
+            device_id=(y, lax.rem(z + k, n_z), s), device_id_type=MESH,
+        )
+
+    @pl.loop(1, n_z)
+    def _(k):
+        vec_copy(k, z).start()
+
+    vec_z[z] = vec[0]
 
     def chain_step(o):
         @pl.loop(0, n_c)
         def _(t):
             c = nth(t)
-            chain_copy(o, c, z, o).wait_recv()
-            part[chunk(o, c), :] = (
+            chain_copy(part, o, c, z, o).wait_recv()
+            rx[chunk(o, c), :] = (
                 part[chunk(o, c), :].astype(F32) + rx[chunk(o, c), :].astype(F32)
             ).astype(BF16)
-            chain_send(o, c)
-
-    def chain_low(k):
-        @pl.when(jnp.logical_and(z - k >= 0, z < n_z - 1))
-        def _():
-            chain_step(z - k)
-
-    def chain_high(k):
-        @pl.when(jnp.logical_and(z + k < n_z, z > 0))
-        def _():
-            chain_step(z + k)
+            chain_send(rx, o, c)
+
+    def chain_low():
+        @pl.loop(1, n_z)
+        def _(k):
+            @pl.when(jnp.logical_and(z - k >= 0, z < n_z - 1))
+            def _():
+                chain_step(z - k)
+
+    def chain_high():
+        @pl.loop(1, n_z)
+        def _(k):
+            @pl.when(jnp.logical_and(z + k < n_z, z > 0))
+            def _():
+                chain_step(z + k)
 
     upper = 2 * z >= n_z
 
-    def cot_step(k):
-        @pl.loop(0, n_c)
-        def _(t):
-            line_step(1, k, nth(t))
-
-    @pl.loop(1, n_z - 1)
-    def _(k):
-        @pl.when(k < n_z - 2)
-        def _():
-            cot_step(k)
-
-            @pl.when(at_end)
-            def _():
-                backward(jnp.where(high_end, z - k, z + k))
-
-        @pl.when(upper)
-        def _():
-            chain_low(k)
-
-        @pl.when(jnp.logical_not(upper))
-        def _():
-            chain_high(k)
-
-    @pl.loop(1, n_z - 1)
-    def _(k):
-        @pl.when(upper)
-        def _():
-            chain_high(k)
-
-        @pl.when(jnp.logical_not(upper))
-        def _():
-            chain_low(k)
-
-    if n_z > 2:
-        cot_step(n_z - 2)
+    @pl.when(upper)
+    def _():
+        chain_low()
+
+    @pl.when(jnp.logical_not(upper))
+    def _():
+        chain_high()
+
+    backward()
+    outs[3].start()
+
+    @pl.when(upper)
+    def _():
+        chain_high()
+
+    @pl.when(jnp.logical_not(upper))
+    def _():
+        chain_low()
 
     def back_copy(k, q, there):
         return pltpu.make_async_remote_copy(
@@ -368,17 +399,16 @@
 
         @pl.when(z < n_z - 1)
         def _():
-            chain_copy(z, c, z, z).wait_recv()
+            chain_copy(part, z, c, z, z).wait_recv()
 
         @pl.when(z > 0)
         def _():
-            chain_copy(z, c, z, n_z).wait_recv()
+            chain_copy(part, z, c, z, n_z).wait_recv()
 
         from_right = jnp.where(z < n_z - 1, rx[chunk(z, c), :].astype(F32), 0.0)
         from_left = jnp.where(z > 0, rx[chunk(n_z, c), :].astype(F32), 0.0)
         final = (part[chunk(z, c), :].astype(F32) + from_right + from_left).astype(BF16)
         back_send[part_rows(c), :] = jnp.dot(expand, final, preferred_element_type=F32).astype(BF16)
-        part[chunk(z, c), :] = final
 
         @pl.loop(0, part_p)
         def _(r):
@@ -389,48 +419,6 @@
                 back_copy(lax.rem(q + n_p - me, n_p), q, me).start()
 
     back[padded_rows(me), :] = back_send[padded_rows(me), :]
-
-    own_rows = rows[0, block(z), :]
-    row_logits = lax.dot_general(
-        own_rows, wr_ref[...], (((1,), (1,)), ((), ())), preferred_element_type=F32
-    )
-    mine = (lax.broadcasted_iota(jnp.int32, row_logits.shape, 1) == me).astype(F32)
-    row_gate = jax.nn.sigmoid(jnp.sum(row_logits * mine, axis=1, keepdims=True))
-    inner = jnp.sum(
-        rows[1, block(z), :].astype(F32) * part[block(z), :].astype(F32), axis=1, keepdims=True
-    )
-    vec[0] = jnp.sum(
-        own_rows.astype(F32) * (inner * (1.0 - row_gate)), axis=0, keepdims=True
-    )
-
-    def vec_copy(k, slot):
-        return pltpu.make_async_remote_copy(
-            src_ref=vec.at[0], dst_ref=vec_z.at[slot], send_sem=v_send.at[k], recv_sem=v_recv.at[k],
-            device_id=(y, lax.rem(z + k, n_z), s), device_id_type=MESH,
-        )
-
-    @pl.loop(1, n_z)
-    def _(k):
-        vec_copy(k, z).start()
-
-    @pl.when(inside)
-    def _():
-        @pl.loop(1, n_z - 1)
-        def _(k):
-            @pl.when(z - k >= 0)
-            def _():
-                backward(z - k)
-
-            @pl.when(z + k < n_z)
-            def _():
-                backward(z + k)
-
-    if n_z > 2:
-        @pl.when(at_end)
-        def _():
-            backward(jnp.where(high_end, 1, n_z - 2))
-
-    vec_z[z] = vec[0]
 
     @pl.loop(1, n_z)
     def _(k):
@@ -457,23 +445,12 @@
     )
     moe_ref[...] = (gate * picked).astype(BF16)
 
-    @pl.loop(0, n_c)
-    def _(t):
-        line_step(1, n_z - 1, nth(t))
-
-    outs[2].start()
-
-    @pl.when(at_end)
-    def _():
-        backward(jnp.where(high_end, 0, n_z - 1))
-
-    outs[3].start()
-
     @pl.loop(1, n_p)
     def _(k):
         vec_plane(k, source(k)).wait_recv()
 
-    router_ref[...] = vec_p[...]
+    for q in range(n_p):
+        router_ref[q : q + 1, :] = vec_p[q]
 
     @pl.loop(1, n_p)
     def _(k):
@@ -502,10 +479,62 @@
 
             @pl.when(o != z)
             def _():
-                chain_copy(o, c, z, o).wait_send()
+                chain_copy(part, o, c, z, o).wait_send()
 
     for out in outs:
         out.wait()
+
+
+def gradient_kernel(
+    scale,
+    rows_hbm, hg_hbm, act_hbm, cots_hbm, moe_hbm, router_hbm,
+    grad_in, grad_out, moe_out, router_out,
+    rows, cots, act, hg, gin, gout, moe, router, in_sem, out_sem,
+):
+    loads = [
+        pltpu.make_async_copy(act_hbm, act, in_sem.at[0]),
+        pltpu.make_async_copy(cots_hbm, cots, in_sem.at[1]),
+        pltpu.make_async_copy(rows_hbm, rows, in_sem.at[2]),
+        pltpu.make_async_copy(hg_hbm, hg, in_sem.at[3]),
+        pltpu.make_async_copy(moe_hbm, moe, in_sem.at[4]),
+        pltpu.make_async_copy(router_hbm, router, in_sem.at[5]),
+    ]
+    for load in loads:
+        load.start()
+    stores = []
+
+    def product(left, right, held, out, sem):
+        count = left.shape[1]
+        half = count // 2 if count % 256 == 0 else count
+        for at in range(0, count, half):
+            held[at : at + half, :] = (
+                lax.dot_general(
+                    left[:, at : at + half], right[...], (((0,), (0,)), ((), ())),
+                    preferred_element_type=F32,
+                )
+                * scale
+            ).astype(BF16)
+            stores.append(
+                pltpu.make_async_copy(
+                    held.at[at : at + half], out.at[at : at + half], out_sem.at[sem + at // half]
+                )
+            )
+            stores[-1].start()
+
+    loads[0].wait()
+    loads[1].wait()
+    product(act, cots, gout, grad_out, 0)
+    loads[4].wait()
+    stores.append(pltpu.make_async_copy(moe, moe_out, out_sem.at[4]))
+    stores[-1].start()
+    loads[5].wait()
+    stores.append(pltpu.make_async_copy(router, router_out, out_sem.at[5]))
+    stores[-1].start()
+    loads[2].wait()
+    loads[3].wait()
+    product(rows, hg, gin, grad_in, 2)
+    for store in stores:
+        store.wait()
 
 
 def shards(tokens, routes, w_router, w_in, w_out, cotangent):
@@ -528,7 +557,7 @@
         functools.partial(exchange_kernel, (n_y, n_z, n_s, cap, capp, blk, n_c, scale)),
         out_shape=(
             jax.ShapeDtypeStruct((tok_count, width), BF16),
-            jax.ShapeDtypeStruct((n_p, 1, width), F32),
+            jax.ShapeDtypeStruct((n_p, width), F32),
             jax.ShapeDtypeStruct((total, width), BF16),
             jax.ShapeDtypeStruct((total, width), BF16),
             jax.ShapeDtypeStruct((total, hidden), BF16),
@@ -563,14 +592,30 @@
             collective_id=0, has_side_effects=True, vmem_limit_bytes=60 << 20
         ),
     )(tokens, routes.reshape(1, tok_count), w_router.T, cotangent, w_in[0], w_out[0])
-    by_row = (((0,), (0,)), ((), ()))
-    grad_in = (
-        lax.dot_general(rows, hg, by_row, preferred_element_type=F32) * scale
-    ).astype(BF16)
-    grad_out = (
-        lax.dot_general(act, cots, by_row, preferred_element_type=F32) * scale
-    ).astype(BF16)
-    return (moe, router[:, 0, :].T, grad_in[None], grad_out[None])
+    grad_in, grad_out, moe, router = pl.pallas_call(
+        functools.partial(gradient_kernel, scale),
+        out_shape=(
+            jax.ShapeDtypeStruct((width, hidden), BF16),
+            jax.ShapeDtypeStruct((hidden, width), BF16),
+            jax.ShapeDtypeStruct((tok_count, width), BF16),
+            jax.ShapeDtypeStruct((n_p, width), F32),
+        ),
+        in_specs=[hbm] * 6,
+        out_specs=(hbm, hbm, hbm, hbm),
+        scratch_shapes=[
+            pltpu.VMEM((total, width), BF16),
+            pltpu.VMEM((total, width), BF16),
+            pltpu.VMEM((total, hidden), BF16),
+            pltpu.VMEM((total, hidden), BF16),
+            pltpu.VMEM((width, hidden), BF16),
+            pltpu.VMEM((hidden, width), BF16),
+            pltpu.VMEM((tok_count, width), BF16),
+            pltpu.VMEM((n_p, width), F32),
+            dma((6,)), dma((6,)),
+        ],
+        compiler_params=pltpu.CompilerParams(vmem_limit_bytes=60 << 20),
+    )(rows, hg, act, cots, moe, router)
+    return (moe, router.T, grad_in[None], grad_out[None])
 
 
 def solution(mesh):

time: 75.1 us -> 66.8 us (0.89)
  matrix products: 8.87 us -> 0 us
  Pallas kernels: 63.2 us -> 66 us
  local copies, waits for them, and re-layouts: 2.13 us -> 0 us
    dot_general x2 -> x0, matrix products: 8.87 us -> none  [the longest x1 5.25 us: shards(): lax.dot_general(rows, hg, by_row, preferred_element_type=F32) * scale]
    pallas_call x0 -> x1, Pallas kernels: none -> 6.58 us  [shards(): pl.pallas_call(functools.partial(gradient_kernel, scale), out_shape=(jax....]
    pallas_call x1, Pallas kernels: 63.2 us -> 59.4 us  [shards(): pl.pallas_call(functools.partial(exchange_kernel, (n_y, n_z, n_s, cap, ca...]
    unnamed x8 -> x0, local copies, waits for them, and re-layouts: 2.13 us -> none
where the time goes in v1:
time: 66.8 us; the launch traced here: 66.7 us
  Pallas kernels  66 us (99%)
    pallas_call x1, Pallas kernels, shards(): pl.pallas_call(functools.partial(exchange_kernel, (n_y, n_z, n_s, cap, ca...  59.4 us
    pallas_call x1, Pallas kernels, shards(): pl.pallas_call(functools.partial(gradient_kernel, scale), out_shape=(jax....  6.58 us

profile of v1, /device:TPU:0, one launch (start us, length us, event | category | flops | bytes accessed | tf_op | source)
XLA Modules:
  0.0 66.7 jit_solution(17837792586688147292)
XLA Ops:
  0.6 59.4 %shard_map.93 = (bf16[128,1280]{1,0:T(8,128)(2,1)}, f32[8,1280]{1,0:T(8,128)}, bf16[384,1280]{1,0:T(8,128)(2,1)}, bf16[384,1280]{1,0:T(8,128)(2,1)}, bf16[384,12...) custom-call(bf16[128,1280]{1,0:T(8,128)(2,1)} %tok_ref.1, s32[1,128]{1,0:T(1,128)} %bitcast.10, bf16[8,1280]{1,0:T(8,128)(2,1)} %bitcast.9, ...), custom_call_target="tpu_custom_call" | custom-call | tf_op jit(solution)/shard_map/pallas_call | solution.py:556
  60.1 6.6 %shard_map.94 = (bf16[1280,1280]{1,0:T(8,128)(2,1)}, bf16[1280,1280]{1,0:T(8,128)(2,1)}, bf16[128,1280]{1,0:T(8,128)(2,1)}, f32[8,1280]{1,0:T(8,128)}) custom-call(bf16[384,1280]{1,0:T(8,128)(2,1)} %get-tuple-element.14.rows_hbm, bf16[384,1280]{1,0:T(8,128)(2,1)} %get-tuple-element.15.hg_hbm, bf16[384,1280]{1,0:T(8,128)(2,1)} %get-tuple-element.16.act_hbm, ...), custom_call_target="tpu_custom_call" | custom-call | tf_op jit(solution)/shard_map/pallas_call | solution.py:595
